TPU v7x, 32 devices: a whole 2x2x4 slice. The times are simulated.
32 devices in a mesh: groups: 2 (over x), seq: 8 (over z, y), role: 2 (over core).
Axes of the slice: x: 2, y: 2, z: 4, core: 2. Of those that a mesh axis runs over, the one named last changes fastest.
Arguments:
- pair_rep: bfloat16 [512, 256, 128], P(('groups', 'seq', 'role')), parts along dimension 0, may hold values from -6 to 6
- tri_gain: float32 [2, 128], replicated, may hold values from 0.1 to 1.9
- tri_proj: bfloat16 [2, 128, 512], replicated, may hold values from -0.5 to 0.5
- tri_gate: bfloat16 [2, 128, 128], replicated, may hold values from -0.5 to 0.5
- tri_mid_gain: float32 [2, 128], replicated, may hold values from 0.1 to 1.9
- tri_out: bfloat16 [2, 128, 128], replicated, may hold values from -0.5 to 0.5
- trans_gain: float32 [128], replicated, may hold values from 0.1 to 1.9
- trans_up: bfloat16 [128, 1024], replicated, may hold values from -0.5 to 0.5
- trans_down: bfloat16 [512, 128], replicated, may hold values from -0.25 to 0.25
Outputs:
- pair_out: bfloat16 [512, 256, 128], P(('groups', 'seq', 'role')), parts along dimension 0
There are 2 independent parts, one for each index of `groups`. A program takes and returns all parts, laid end to end along the dimension named above; an argument that names none is the same for every part. Nothing has to cross between parts.
All inputs are finite; a program needn't handle non-finite values.
Results may differ from a plain program's by a relative error of at most 0.012.
Values may be sent and summed in bfloat16 or wider, within the bound.
A program may use at most 64 MiB of HBM per device.

v0:
```python
import math

import jax
import jax.numpy as jnp
from jax import lax
from jax.sharding import PartitionSpec as P

epsilon = 1e-05


def layer_norm(values, gain):
    average = jnp.mean(values, axis=-1, keepdims=True)
    centred = values - average
    spread = jnp.mean(centred * centred, axis=-1, keepdims=True)
    return centred * lax.rsqrt(spread + epsilon) * gain


def multiply(left_side, right_side, which):
    if which == 0:
        return jnp.einsum("cik,cjk->cij", left_side, right_side, preferred_element_type=jnp.float32)
    return jnp.einsum("cki,ckj->cij", left_side, right_side, preferred_element_type=jnp.float32)


def local(
    pair_rep, tri_gain, tri_proj, tri_gate, tri_mid_gain, tri_out, trans_gain, trans_up, trans_down
):
    rows, width, channels = pair_rep.shape
    inner = tri_out.shape[1]
    hidden_width = trans_down.shape[0]
    seq_count = lax.axis_size("seq")
    role_count = lax.axis_size("role")
    groups_total = seq_count * role_count
    per_device = inner // groups_total
    block_rows = math.gcd(rows, 4)
    current = pair_rep
    for which in range(2):
        pieces = []
        gate_list = []
        for start_row in range(0, rows, block_rows):
            block_in = current[start_row : start_row + block_rows].astype(jnp.float32)
            normed = layer_norm(block_in, tri_gain[which]).astype(jnp.bfloat16)
            projected = jnp.einsum(
                "rnd,de->ern", normed, tri_proj[which], preferred_element_type=jnp.float32
            )
            left_side = projected[:inner] * jax.nn.sigmoid(projected[inner : 2 * inner])
            right_side = projected[2 * inner : 3 * inner] * jax.nn.sigmoid(projected[3 * inner :])
            pieces.append(jnp.stack([left_side, right_side]).astype(jnp.bfloat16))
            gate_list.append(
                jax.nn.sigmoid(
                    jnp.einsum(
                        "rnd,de->rne", normed, tri_gate[which], preferred_element_type=jnp.float32
                    )
                )
            )
        stacked = jnp.concatenate(pieces, axis=2)
        gating = jnp.concatenate(gate_list, axis=0)
        sending = stacked.reshape(2, groups_total, per_device, 1, rows, width)

        def product_fn(arrived, which=which):
            count_items = arrived.shape[2]
            whole = arrived.reshape(2, count_items, width, width)
            result = multiply(whole[0], whole[1], which).astype(jnp.bfloat16)
            return result.reshape(1, count_items, width, width)

        result = product_fn(
            lax.all_to_all(sending, ("seq", "role"), split_axis=1, concat_axis=3, tiled=True)
        )
        returned = lax.all_to_all(
            result.reshape(1, per_device, groups_total, rows, width),
            ("seq", "role"),
            split_axis=2,
            concat_axis=0,
            tiled=True,
        )
        mixed = returned.reshape(inner, rows, width).astype(jnp.float32)
        average = jnp.mean(mixed, axis=0, keepdims=True)
        centred = mixed - average
        spread = jnp.mean(centred * centred, axis=0, keepdims=True)
        normed_mid = (
            centred * lax.rsqrt(spread + epsilon) * tri_mid_gain[which][:, None, None]
        ).astype(jnp.bfloat16)
        update = jnp.einsum(
            "crn,ce->rne", normed_mid, tri_out[which], preferred_element_type=jnp.float32
        )
        current = (current.astype(jnp.float32) + gating * update).astype(jnp.bfloat16)
    outputs = []
    for start_row in range(0, rows, block_rows):
        block_in = current[start_row : start_row + block_rows].astype(jnp.float32)
        normed = layer_norm(block_in, trans_gain).astype(jnp.bfloat16)
        values = jnp.einsum("rnd,de->rne", normed, trans_up, preferred_element_type=jnp.float32)
        hidden = (jax.nn.silu(values[..., :hidden_width]) * values[..., hidden_width:]).astype(
            jnp.bfloat16
        )
        down = jnp.einsum("rnd,de->rne", hidden, trans_down, preferred_element_type=jnp.float32)
        outputs.append((block_in + down).astype(jnp.bfloat16))
    return jnp.concatenate(outputs, axis=0)


def solution(mesh):
    in_specs = (P(("groups", "seq", "role"), None, None), P(), P(), P(), P(), P(), P(), P(), P())
    out_specs = P(("groups", "seq", "role"), None, None)
    return jax.shard_map(local, mesh=mesh, in_specs=in_specs, out_specs=out_specs, check_vma=False)
```

profile of v0, /device:TPU:5, one launch (start us, length us, event | category | flops | bytes accessed | tf_op | source)
XLA Modules:
  0.0 202.9 jit_solution(14559246247579466240)
XLA Ops:
  0.0 1.7 convert_reduce_fusion.11
  1.7 2.4 %fusion.113 = (f32[4,256]{1,0:T(4,128)S(1)}, f32[4,256]{1,0:T(4,128)S(1)}, f32[4,256]{1,0:T(4,128)S(1)}, f32[4,256]{1,0:T(4,128)S(1)}) fusion(f32[4,256]{1,0:T(4,128)S(1)} %get-tuple-element.56, bf16[16,256,128]{2,1,0:T(8,128)(2,1)} %param.9, f32[4,256]{1,0:T(4,128)S(1)} %get-tuple-element.55, f32[4,256]{1,0:T(4,128)S(1)} %get-tuple-element.54, ...), kind=kLoop, calls=%fused_computation.167 | loop fusion | flops 2093056 | bytes 1081344 | tf_op jit(solution)/shard_map/reduce_sum | solution.py:14
  4.2 0.5 convolution_bitcast_fusion.5
  4.7 0.3 fusion.184
  5.3 0.5 convolution_bitcast_fusion.4
  5.8 0.3 fusion.186
  6.4 0.5 convolution_bitcast_fusion.6
  6.9 0.3 fusion.182
  7.3 0.5 convolution_bitcast_fusion.7
  7.8 1.1 fusion.180
  8.9 1.1 copy.89
  9.9 1.8 copy.90
  11.7 0.8 copy.91
  12.6 1.2 maximum_maximum_fusion
  13.8 0.2 copy.97
  14.1 53.8 %all_to_all.48 = bf16[2,16,8,1,16,256]{5,2,4,3,0,1:T(8,128)(2,1)S(1)} all-to-all(bf16[2,16,8,1,16,256]{5,2,4,3,0,1:T(8,128)(2,1)S(1)} %copy.97), channel_id=1, replica_groups=mesh['groups'=2,'seq'=8,'role'=2] {'seq','role'}, dimensions={1} | all-to-all | bytes 4194304 | tf_op jit(solution)/shard_map/all_to_all | solution.py:66
  68.5 0.5 convolution_convert_fusion.1
  69.0 1.1 copy.100
  70.1 5.1 %all-to-all-start.1 = ((bf16[1,8,16,16,256]{4,3,1,0,2:T(8,128)(2,1)}), bf16[1,8,16,16,256]{4,3,1,0,2:T(8,128)(2,1)S(1)}, u32[]{:S(2)}, u32[]{:S(2)}) async-start(bf16[1,8,16,16,256]{4,3,1,0,2:T(8,128)(2,1)} %copy.100), calls=%async_computation.1 | async-start | bytes 2097152 | tf_op jit(solution)/shard_map/all_to_all | solution.py:68
  75.2 1.3 copy.87
  76.6 0.9 fusion.39
  77.5 1.4 fusion.42
  78.9 1.4 fusion.45
  80.3 1.4 fusion.36
  81.7 17.0 %all-to-all-done.1 = bf16[1,8,16,16,256]{4,3,1,0,2:T(8,128)(2,1)S(1)} async-done(((bf16[1,8,16,16,256]{4,3,1,0,2:T(8,128)(2,1)}), bf16[1,8,16,16,256]{4,3,1,0,2:T(8,128)(2,1)S(1)}, u32[]{:S(2)}, u32[]{:S(2)}) %all-to-all-start.1) | async-done | bytes 1048608 | tf_op jit(solution)/shard_map/all_to_all | solution.py:68
  98.9 0.3 fusion.19
  99.3 0.3 fusion.21
  99.6 0.3 copy-done.3
  100.4 0.6 fusion.5
  101.2 0.3 fusion.101
  101.6 0.5 convolution_bitcast_fusion.3
  102.1 0.3 fusion.188
  102.7 0.5 convolution_bitcast_fusion.2
  103.2 0.3 fusion.190
  103.8 0.5 convolution_bitcast_fusion.1
  104.4 0.3 fusion.192
  105.0 0.5 convolution_bitcast_fusion
  105.5 1.0 fusion.194
  106.6 1.1 copy.119
  107.7 0.3 maximum_maximum_fusion.1
  108.0 0.2 copy.120
  108.3 53.3 %all_to_all.49 = bf16[2,16,8,1,16,256]{5,2,4,3,0,1:T(8,128)(2,1)S(1)} all-to-all(bf16[2,16,8,1,16,256]{5,2,4,3,0,1:T(8,128)(2,1)S(1)} %copy.120), channel_id=1, replica_groups=mesh['groups'=2,'seq'=8,'role'=2] {'seq','role'}, dimensions={1} | all-to-all | bytes 4194304 | tf_op jit(solution)/shard_map/all_to_all | solution.py:66
  161.6 0.5 copy.161
  162.2 0.5 convolution_convert_fusion
  162.7 1.1 copy.123
  163.8 5.0 %all-to-all-start.3 = ((bf16[1,8,16,16,256]{4,3,1,0,2:T(8,128)(2,1)}), bf16[1,8,16,16,256]{4,3,1,0,2:T(8,128)(2,1)S(1)}, u32[]{:S(2)}, u32[]{:S(2)}) async-start(bf16[1,8,16,16,256]{4,3,1,0,2:T(8,128)(2,1)} %copy.123), calls=%async_computation.3 | async-start | bytes 2097152 | tf_op jit(solution)/shard_map/all_to_all | solution.py:68
  168.9 0.4 fusion.33
  169.2 1.2 fusion.30
  170.4 1.2 fusion.27
  171.6 1.1 fusion.24
  172.7 19.6 %all-to-all-done.3 = bf16[1,8,16,16,256]{4,3,1,0,2:T(8,128)(2,1)S(1)} async-done(((bf16[1,8,16,16,256]{4,3,1,0,2:T(8,128)(2,1)}), bf16[1,8,16,16,256]{4,3,1,0,2:T(8,128)(2,1)S(1)}, u32[]{:S(2)}, u32[]{:S(2)}) %all-to-all-start.3) | async-done | bytes 1048608 | tf_op jit(solution)/shard_map/all_to_all | solution.py:68
  192.5 0.3 fusion.12
  192.9 0.3 fusion.14
  193.6 0.6 fusion.7
  194.5 0.3 fusion.89
  195.0 0.8 fusion.196
  195.8 0.8 fusion.198
  196.7 0.8 fusion.46
  197.5 0.8 fusion.47
  198.3 0.8 fusion.200
  199.1 0.8 fusion.48
  199.9 0.8 fusion.202
  200.7 0.8 fusion.49
  201.6 1.3 copy.134
  (84 shorter events, 4.9 us)
Async XLA Ops:
  0.0 194.9 %copy-start = (bf16[128,1024]{1,0:T(8,128)(2,1)S(1)}, bf16[128,1024]{1,0:T(8,128)(2,1)}, u32[]{:S(2)}) copy-start(bf16[128,1024]{1,0:T(8,128)(2,1)} %param.16) | copy-start | bytes 786436
  0.0 4.2 %copy-start.1 = (bf16[16,256,128]{2,1,0:T(8,128)(2,1)S(1)}, bf16[16,256,128]{2,1,0:T(8,128)(2,1)}, u32[]{:S(2)}) copy-start(bf16[16,256,128]{2,1,0:T(8,128)(2,1)} %param.9) | copy-start | bytes 3145732
  0.0 4.1 %copy-start.5 = (f32[2,128]{1,0:T(2,128)S(1)}, f32[2,128]{1,0:T(2,128)}, u32[]{:S(2)}) copy-start(f32[2,128]{1,0:T(2,128)} %param.10) | copy-start | bytes 3076
  0.0 4.2 %copy-start.2 = (bf16[2,128,512]{2,1,0:T(8,128)(2,1)S(1)}, bf16[2,128,512]{2,1,0:T(8,128)(2,1)}, u32[]{:S(2)}) copy-start(bf16[2,128,512]{2,1,0:T(8,128)(2,1)} %param.11) | copy-start | bytes 786436
  70.1 6.4 %copy-start.6 = (f32[2,128]{1,0:T(2,128)S(1)}, f32[2,128]{1,0:T(2,128)}, u32[]{:S(2)}) copy-start(f32[2,128]{1,0:T(2,128)} %param.13) | copy-start | bytes 3076
  70.1 6.5 %copy-start.8 = (bf16[2,128,128]{2,1,0:T(8,128)(2,1)S(1)}, bf16[2,128,128]{2,1,0:T(8,128)(2,1)}, u32[]{:S(2)}) copy-start(bf16[2,128,128]{2,1,0:T(8,128)(2,1)} %param.12) | copy-start | bytes 196612
  70.1 28.6 %all-to-all-start.1 = ((bf16[1,8,16,16,256]{4,3,1,0,2:T(8,128)(2,1)}), bf16[1,8,16,16,256]{4,3,1,0,2:T(8,128)(2,1)S(1)}, u32[]{:S(2)}, u32[]{:S(2)}) async-start(bf16[1,8,16,16,256]{4,3,1,0,2:T(8,128)(2,1)} %copy.100), calls=%async_computation.1 | async-start | bytes 2097152 | tf_op jit(solution)/shard_map/all_to_all | solution.py:68
  81.7 17.9 %copy-start.9 = (bf16[2,128,128]{2,1,0:T(8,128)(2,1)S(1)}, bf16[2,128,128]{2,1,0:T(8,128)(2,1)}, u32[]{:S(2)}) copy-start(bf16[2,128,128]{2,1,0:T(8,128)(2,1)} %param.14) | copy-start | bytes 196612
  98.7 1.2 copy-start.3
  98.7 1.4 copy-start.11
  98.7 1.5 copy-start.13
  98.7 1.7 copy-start.15
  163.8 28.5 %all-to-all-start.3 = ((bf16[1,8,16,16,256]{4,3,1,0,2:T(8,128)(2,1)}), bf16[1,8,16,16,256]{4,3,1,0,2:T(8,128)(2,1)S(1)}, u32[]{:S(2)}, u32[]{:S(2)}) async-start(bf16[1,8,16,16,256]{4,3,1,0,2:T(8,128)(2,1)} %copy.123), calls=%async_computation.3 | async-start | bytes 2097152 | tf_op jit(solution)/shard_map/all_to_all | solution.py:68
  172.7 20.4 %copy-start.10 = (bf16[2,128,128]{2,1,0:T(8,128)(2,1)S(1)}, bf16[2,128,128]{2,1,0:T(8,128)(2,1)}, u32[]{:S(2)}) copy-start(bf16[2,128,128]{2,1,0:T(8,128)(2,1)} %param.14) | copy-start | bytes 196612
  192.3 1.0 copy-start.12
  192.3 1.2 copy-start.14
  192.3 1.4 copy-start.16
  194.3 0.7 copy-start.4
  195.8 0.9 copy-start.7
where the time goes:
time: 205 us; the launch traced here: 203 us
  blocking collectives  107 us (52%)
  waiting for transfers between devices  36.6 us (18%)
  matrix products  21.6 us (11%)
  local copies, waits for them, and re-layouts  14.7 us (7%)
  other arithmetic  12.3 us (6%)
  starting transfers between devices  10 us (5%)
    all_to_all x2, blocking collectives, local(): lax.all_to_all(sending, ('seq', 'role'), split_axis=1, concat_axis=3, til...  107 us
    all_to_all x2, waiting for transfers between devices, local(): lax.all_to_all(result.reshape(1, per_device, groups_total, rows, width),...  36.6 us
    all_to_all x2, starting transfers between devices, local(): lax.all_to_all(result.reshape(1, per_device, groups_total, rows, width),...  10 us
    dot_general x8, matrix products, local(): jnp.einsum('rnd,de->rne', normed, tri_gate[which], preferred_element_type...  8.95 us
    another operation x16, local copies, waits for them, and re-layouts  6.54 us
  transfers between devices with their start and end apart: 2, of which 2 were waited for; matrix products, arithmetic and copies ran while one was open for 5% of the time, Pallas kernels for 0%

commit v1 on v0

v1 whole, which is shorter than its diff:
```python
import functools

import jax
import jax.numpy as jnp
from jax import lax
from jax.experimental import pallas as pl
from jax.experimental.pallas import tpu as pltpu
from jax.sharding import PartitionSpec as P

epsilon = 1e-05
MESH = pl.DeviceIdType.MESH
LANES = 128
CB = 16


def sigmoid(v):
    return 0.5 * jnp.tanh(0.5 * v) + 0.5


def norm(v, gain, axis):
    average = jnp.mean(v, axis=axis, keepdims=True)
    centred = v - average
    spread = jnp.mean(centred * centred, axis=axis, keepdims=True)
    return (centred * lax.rsqrt(spread + epsilon) * gain).astype(jnp.bfloat16)


def dot(a, b, da, db):
    return lax.dot_general(a, b, (((da,), (db,)), ((), ())), preferred_element_type=jnp.float32)


def kernel(
    N, M, Q, R, roles,
    pair, gain, projT, gatew, midg, outw, tgain, up, down, out,
    lbuf, rbuf, cur1, gates, l0, r0, l1, r1, lT, rT, pT, psend, precv, xsend, xrecv, own,
    ls, lr, rs, rr, l1s, l1r, r1s, r1r, ps, pr, xs, xr,
):
    C = pair.shape[2]
    inner = outw.shape[1]
    hidden = down.shape[0]
    me = lax.axis_index("seq") * roles + lax.axis_index("role")
    q, m = lax.div(me, M), lax.rem(me, M)
    part = M * R

    def where(d):
        return {"seq": lax.div(d, roles), "role": lax.rem(d, roles)}

    def loop(count, body, unroll=1):
        def step(i, carry):
            body(i)
            return carry
        lax.fori_loop(0, count, step, 0, unroll=unroll)

    def lanes(p):
        return pl.ds(pl.multiple_of(p * LANES, LANES), LANES)

    def chans(u):
        return pl.ds(pl.multiple_of(u * CB, CB), CB)

    def rows(u, size):
        return pl.ds(pl.multiple_of(u * size, size), size)

    def remote(src, dst, ssem, rsem, d):
        return pltpu.make_async_remote_copy(
            src_ref=src, dst_ref=dst, send_sem=ssem, recv_sem=rsem,
            device_id=where(d), device_id_type=MESH)

    barrier = pltpu.get_barrier_semaphore()
    def greet(i):
        pl.semaphore_signal(barrier, inc=1, device_id=where(lax.rem(me + 1 + i, N)), device_id_type=MESH)
    loop(N - 1, greet)

    def project(t, cur, p):
        def row(r):
            x = cur[r, lanes(p), :].astype(jnp.float32)
            xn = norm(x, gain[t : t + 1, :], 1)
            pj = dot(projT[t], xn, 1, 1)
            lbuf[t, r, :, lanes(p)] = (pj[:inner] * sigmoid(pj[inner : 2 * inner])).astype(jnp.bfloat16)
            rbuf[t, r, :, lanes(p)] = (pj[2 * inner : 3 * inner] * sigmoid(pj[3 * inner :])).astype(jnp.bfloat16)
            gates[r, lanes(p), :] = sigmoid(dot(xn, gatew[t], 1, 0))
        loop(R, row, 2)

    def left_copy(t, u, p, src):
        dst, s, r_ = (l0, ls, lr) if t == 0 else (l1, l1s, l1r)
        return remote(lbuf.at[t, :, chans(u), lanes(p)], dst.at[rows(src, R), :, lanes(p)],
                      s.at[u, p], r_.at[src, p], q * M + u)

    def right_copy(t, d, p, src):
        if t == 0:
            return remote(rbuf.at[t, :, chans(lax.rem(d, M)), lanes(p)], r0.at[rows(src, R), :, lanes(p)],
                          rs.at[d, p], rr.at[src, p], d)
        return remote(rbuf.at[t, :, chans(d), lanes(p)], r1.at[rows(src, R), :, lanes(p)],
                      r1s.at[d, p], r1r.at[src, p], q * M + d)

    def self_copies(t, p):
        dl, sl = (l0, lr) if t == 0 else (l1, l1r)
        dr, sr, at = (r0, rr, me) if t == 0 else (r1, r1r, m)
        return (pltpu.make_async_copy(lbuf.at[t, :, chans(m), lanes(p)], dl.at[rows(m, R), :, lanes(p)], sl.at[m, p]),
                pltpu.make_async_copy(rbuf.at[t, :, chans(m), lanes(p)], dr.at[rows(at, R), :, lanes(p)], sr.at[at, p]))

    def send_lr(t, p):
        for c in self_copies(t, p):
            c.start()
        def near(i):
            u = lax.rem(m + 1 + i, M)
            left_copy(t, u, p, m).start()
            right_copy(t, q * M + u if t == 0 else u, p, me if t == 0 else m).start()
        if t == 0:
            def far(i):
                d = lax.rem(q + 1 + lax.div(i, M), Q) * M + lax.rem(m + i, M)
                right_copy(0, d, p, me).start()
            loop(N - M, far)
        loop(M - 1, near)

    def swap(x):
        return jnp.swapaxes(x, 0, 1)

    def back_copy(t, u, p, src):
        return remote(psend.at[t, p, u], precv.at[t, :, chans(src), lanes(p)],
                      ps.at[t, u, p], pr.at[t, src, p], q * M + u)

    def send_back(t, p):
        def one(u):
            psend[t, p, u] = swap(pT[:, rows(u, R), :])
        loop(M, one)
        pltpu.make_async_copy(psend.at[t, p, m], precv.at[t, :, chans(m), lanes(p)], pr.at[t, m, p]).start()
        def go(i):
            back_copy(t, lax.rem(m + 1 + i, M), p, m).start()
        loop(M - 1, go)

    def wait_back(t, p):
        def one(u):
            pltpu.make_async_copy(psend.at[t, p, u], precv.at[t, :, chans(u), lanes(p)], pr.at[t, u, p]).wait()
        loop(M, one)

    def updated(t, cur, r, p):
        y = precv[t, r, :, lanes(p)].astype(jnp.float32)
        yn = norm(y, midg[t], 0)
        upd = dot(yn, outw[t], 0, 0)
        return (cur[r, lanes(p), :].astype(jnp.float32) + gates[r, lanes(p), :] * upd).astype(jnp.bfloat16)

    for s in range(Q):
        project(0, pair, s)
        if s == 0:
            pl.semaphore_wait(barrier, N - 1)
        send_lr(0, s)
    for s in range(Q):
        p = lax.rem(q + s, Q)
        def arrive(u, s=s, p=p):
            at = p * M + u
            for h in range(Q):
                pltpu.make_async_copy(rbuf.at[0, :, chans(u), lanes(h)], r0.at[rows(at, R), :, lanes(h)], rr.at[at, h]).wait()
                if s == 0:
                    pltpu.make_async_copy(lbuf.at[0, :, chans(u), lanes(h)], l0.at[rows(u, R), :, lanes(h)], lr.at[u, h]).wait()
            rT[:, rows(u, R), :] = swap(r0[rows(at, R)])
            if s == 0:
                lT[:, rows(u, R), :] = swap(l0[rows(u, R)])
        loop(M, arrive)
        def product(c):
            pT[c] = dot(lT[c], rT[c], 1, 1).astype(jnp.bfloat16)
        loop(CB, product, 2)
        send_back(0, p)
    for s in range(Q):
        p = lax.rem(q + s, Q)
        wait_back(0, p)
        def row(r, p=p):
            cur1[r, lanes(p), :] = updated(0, pair, r, p)
        loop(R, row, 2)
        project(1, cur1, p)
        send_lr(1, p)
    def arrive1(u):
        for h in range(Q):
            pltpu.make_async_copy(rbuf.at[1, :, chans(u), lanes(h)], r1.at[rows(u, R), :, lanes(h)], r1r.at[u, h]).wait()
            pltpu.make_async_copy(lbuf.at[1, :, chans(u), lanes(h)], l1.at[rows(u, R), :, lanes(h)], l1r.at[u, h]).wait()
        rT[:, rows(u, R), :] = swap(r1[rows(u, R)])
        lT[:, rows(u, R), :] = swap(l1[rows(u, R)])
    loop(M, arrive1)

    def cross(d, p):
        return remote(xsend.at[d - 1, p], xrecv.at[d - 1, p], xs.at[d - 1, p], xr.at[d - 1, p],
                      lax.rem(q + d, Q) * M + m)

    for p in range(Q):
        for d in range(1, Q):
            other = lax.rem(q + d, Q)
            def partial(c, d=d, p=p, other=other):
                xsend[d - 1, p, c] = dot(lT[c, :, lanes(other)], rT[c, :, lanes(p)], 0, 0).astype(jnp.bfloat16)
            loop(CB, partial, 2)
            cross(d, p).start()
    for p in range(Q):
        def mine(c, p=p):
            own[p, c] = dot(lT[c, :, lanes(q)], rT[c, :, lanes(p)], 0, 0)
        loop(CB, mine, 2)
    for p in range(Q):
        for d in range(1, Q):
            cross(d, p).wait_recv()
        def total(c, p=p):
            v = own[p, c]
            for d in range(1, Q):
                v = v + xrecv[d - 1, p, c].astype(jnp.float32)
            pT[c] = v.astype(jnp.bfloat16)
        loop(CB, total, 2)
        send_back(1, p)
    for p in range(Q):
        wait_back(1, p)
        def last(r, p=p):
            cur = updated(1, cur1, r, p).astype(jnp.float32)
            xn = norm(cur, tgain[...], 1)
            val = dot(xn, up[...], 1, 0)
            q0, q1 = val[:, :hidden], val[:, hidden:]
            h = (q0 * sigmoid(q0) * q1).astype(jnp.bfloat16)
            out[r, lanes(p), :] = (cur + dot(h, down[...], 1, 0)).astype(jnp.bfloat16)
        loop(R, last, 2)
    def drain(i):
        u = lax.rem(m + 1 + i, M)
        for p in range(Q):
            left_copy(0, u, p, m).wait_send()
            left_copy(1, u, p, m).wait_send()
            right_copy(1, u, p, m).wait_send()
            for t in range(2):
                back_copy(t, u, p, m).wait_send()
    loop(M - 1, drain)
    def drain_right(i):
        d = lax.rem(me + 1 + i, N)
        for p in range(Q):
            right_copy(0, d, p, me).wait_send()
    loop(N - 1, drain_right)
    for p in range(Q):
        for d in range(1, Q):
            cross(d, p).wait_send()


def solution(mesh):
    N = mesh.shape["seq"] * mesh.shape["role"]
    roles = mesh.shape["role"]

    def local(pair, tri_gain, tri_proj, tri_gate, tri_mid_gain, tri_out, trans_gain, trans_up, trans_down):
        R, W, C = pair.shape
        inner = tri_out.shape[1]
        M = inner // CB
        Q = N // M
        bf, f32, vm, dma = jnp.bfloat16, jnp.float32, pltpu.VMEM, pltpu.SemaphoreType.DMA
        part = M * R
        assert part == LANES and Q * LANES == W
        X = max(Q - 1, 1)
        return pl.pallas_call(
            functools.partial(kernel, N, M, Q, R, roles),
            out_shape=jax.ShapeDtypeStruct((R, W, C), bf),
            in_specs=[pl.BlockSpec(memory_space=vm)] * 9,
            out_specs=pl.BlockSpec(memory_space=vm),
            scratch_shapes=[
                vm((2, R, inner, W), bf), vm((2, R, inner, W), bf),
                vm((R, W, C), bf), vm((R, W, C), f32),
                vm((part, CB, W), bf), vm((W, CB, W), bf),
                vm((part, CB, W), bf), vm((part, CB, W), bf),
                vm((CB, part, W), bf), vm((CB, part, W), bf), vm((CB, part, LANES), bf),
                vm((2, Q, M, R, CB, LANES), bf), vm((2, R, inner, W), bf),
                vm((X, Q, CB, part, LANES), bf), vm((X, Q, CB, part, LANES), bf),
                vm((Q, CB, part, LANES), f32),
                dma((M, Q)), dma((M, Q)), dma((N, Q)), dma((N, Q)),
                dma((M, Q)), dma((M, Q)), dma((M, Q)), dma((M, Q)),
                dma((2, M, Q)), dma((2, M, Q)), dma((X, Q)), dma((X, Q)),
            ],
            compiler_params=pltpu.CompilerParams(
                collective_id=0, has_side_effects=True, vmem_limit_bytes=66_000_000),
        )(pair, tri_gain, jnp.swapaxes(tri_proj, 1, 2), tri_gate, tri_mid_gain[:, :, None], tri_out,
          trans_gain[None, :], trans_up, trans_down)

    in_specs = (P(("groups", "seq", "role"), None, None), P(), P(), P(), P(), P(), P(), P(), P())
    out_specs = P(("groups", "seq", "role"), None, None)
    return jax.shard_map(local, mesh=mesh, in_specs=in_specs, out_specs=out_specs, check_vma=False)
```

time: 205 us -> 174 us (0.85)
  Pallas kernels: 0 us -> 168 us
  blocking collectives: 107 us -> 0 us
  waiting for transfers between devices: 36.6 us -> 0 us
  matrix products: 21.6 us -> 0 us
  other arithmetic: 12.3 us -> 0 us
  starting transfers between devices: 10 us -> 0 us
  local copies, waits for them, and re-layouts: 14.7 us -> 5.56 us
    pallas_call x0 -> x1, Pallas kernels: none -> 168 us  [local(): pl.pallas_call(functools.partial(kernel, N, M, Q, R, roles), out_shape=ja...]
    all_to_all x2 -> x0, blocking collectives: 107 us -> none  [local(): lax.all_to_all(sending, ('seq', 'role'), split_axis=1, concat_axis=3, til...]
    all_to_all x2 -> x0, waiting for transfers between devices: 36.6 us -> none  [local(): lax.all_to_all(result.reshape(1, per_device, groups_total, rows, width),...]
    dot_general x28 -> x0, matrix products: 21.6 us -> none  [the longest x8 8.95 us: local(): jnp.einsum('rnd,de->rne', normed, tri_gate[which], preferred_element_type...]
    all_to_all x2 -> x0, starting transfers between devices: 10 us -> none  [local(): lax.all_to_all(result.reshape(1, per_device, groups_total, rows, width),...]
    another operation x18 -> x0, local copies, waits for them, and re-layouts: 8.71 us -> none
    reduce_sum x10 -> x0, other arithmetic: 6.12 us -> none  [the longest x3 3.04 us: layer_norm(): spread = jnp.mean(centred * centred, axis=-1, keepdims=True)]
    another operation x8 -> x0, other arithmetic: 3.74 us -> none
  transfers between devices with their start and end apart: 2 -> 0, of which waited for: 2 -> 0; matrix products, arithmetic and copies ran while one was open for 5% -> 0% of each run, Pallas kernels for 0% -> 0%
where the time goes in v1:
time: 174 us
  Pallas kernels  168 us (97%)
  local copies, waits for them, and re-layouts  5.56 us (3%)
    pallas_call x1, Pallas kernels, local(): pl.pallas_call(functools.partial(kernel, N, M, Q, R, roles), out_shape=ja...  168 us
    unnamed x4, local copies, waits for them, and re-layouts  4.76 us

profile of v1, /device:TPU:5, one launch (start us, length us, event | category | flops | bytes accessed | tf_op | source)
XLA Modules:
  0.0 173.7 jit_solution(883890027645588540)
XLA Ops:
  0.0 0.0 copy-start
  0.0 0.7 copy-done
  0.7 0.8 copy.12.midg
  1.5 1.8 %copy.11 = bf16[2,128,512]{1,2,0:T(8,128)(2,1)} copy(bf16[2,128,512]{2,1,0:T(8,128)(2,1)} %param.11) | data formatting | bytes 524288 | tf_op args[2]
  3.3 168.2 %shard_map.91 = bf16[16,256,128]{2,1,0:T(8,128)(2,1)} custom-call(bf16[16,256,128]{2,1,0:T(8,128)(2,1)} %pair.1, f32[2,128]{1,0:T(2,128)} %gain.1, bf16[2,512,128]{2,1,0:T(8,128)(2,1)} %bitcast.3, bf16[2,128,128]{2,1,0:T(8,128)(2,1)} %gatew.1, f32[2,128,1]{2,1,0:T(8,128)} %copy.12.midg, bf16[2,128,128]{2,1,0:T(8,128)(2,1)} %outw.1, f32[1,128]{1,0:T(1,128)} %bitcast.5, ...), custom_call_target="tpu_custom_call" | custom-call | tf_op jit(solution)/shard_map/pallas_call | solution.py:245
  171.4 2.3 %copy.14 = bf16[16,256,128]{2,1,0:T(8,128)(2,1)} copy(bf16[16,256,128]{2,1,0:T(8,128)(2,1)} %shard_map.91) | data formatting | bytes 2097152
Async XLA Ops:
  0.0 0.7 copy-start

commit v2 on v1

--- a/solution.py
+++ b/solution.py
@@ -10,6 +10,7 @@
 epsilon = 1e-05
 MESH = pl.DeviceIdType.MESH
 LANES = 128
+G = 4
 CB = 16
 
 
@@ -69,15 +70,19 @@
         pl.semaphore_signal(barrier, inc=1, device_id=where(lax.rem(me + 1 + i, N)), device_id_type=MESH)
     loop(N - 1, greet)
 
+    def tokens(cur, r, p):
+        return cur[pl.ds(r * G, G), lanes(p), :].astype(jnp.float32).reshape(G * LANES, C)
+
     def project(t, cur, p):
         def row(r):
-            x = cur[r, lanes(p), :].astype(jnp.float32)
-            xn = norm(x, gain[t : t + 1, :], 1)
-            pj = dot(projT[t], xn, 1, 1)
-            lbuf[t, r, :, lanes(p)] = (pj[:inner] * sigmoid(pj[inner : 2 * inner])).astype(jnp.bfloat16)
-            rbuf[t, r, :, lanes(p)] = (pj[2 * inner : 3 * inner] * sigmoid(pj[3 * inner :])).astype(jnp.bfloat16)
-            gates[r, lanes(p), :] = sigmoid(dot(xn, gatew[t], 1, 0))
-        loop(R, row, 2)
+            xn = norm(tokens(cur, r, p), gain[t : t + 1, :], 1)
+            gates[pl.ds(r * G, G), lanes(p), :] = sigmoid(dot(xn, gatew[t], 1, 0)).reshape(G, LANES, C)
+            for buf, at in ((lbuf, 0), (rbuf, 2 * inner)):
+                pj = dot(projT[t, at : at + 2 * inner], xn, 1, 1)
+                v = (pj[:inner] * sigmoid(pj[inner:])).astype(jnp.bfloat16)
+                for g in range(G):
+                    buf[t, r * G + g, :, lanes(p)] = v[:, g * LANES : (g + 1) * LANES]
+        loop(R // G, row)
 
     def left_copy(t, u, p, src):
         dst, s, r_ = (l0, ls, lr) if t == 0 else (l1, l1s, l1r)
@@ -100,16 +105,19 @@
     def send_lr(t, p):
         for c in self_copies(t, p):
             c.start()
-        def near(i):
+        def near_left(i):
+            left_copy(t, lax.rem(m + 1 + i, M), p, m).start()
+        def near_right(i):
             u = lax.rem(m + 1 + i, M)
-            left_copy(t, u, p, m).start()
             right_copy(t, q * M + u if t == 0 else u, p, me if t == 0 else m).start()
-        if t == 0:
-            def far(i):
-                d = lax.rem(q + 1 + lax.div(i, M), Q) * M + lax.rem(m + i, M)
-                right_copy(0, d, p, me).start()
-            loop(N - M, far)
-        loop(M - 1, near)
+        loop(M - 1, near_left)
+        loop(M - 1, near_right)
+
+    def send_far(p):
+        def far(i):
+            d = lax.rem(q + 1 + lax.div(i, M), Q) * M + lax.rem(m + i, M)
+            right_copy(0, d, p, me).start()
+        loop(N - M, far)
 
     def swap(x):
         return jnp.swapaxes(x, 0, 1)
@@ -132,17 +140,32 @@
             pltpu.make_async_copy(psend.at[t, p, u], precv.at[t, :, chans(u), lanes(p)], pr.at[t, u, p]).wait()
         loop(M, one)
 
-    def updated(t, cur, r, p):
-        y = precv[t, r, :, lanes(p)].astype(jnp.float32)
-        yn = norm(y, midg[t], 0)
-        upd = dot(yn, outw[t], 0, 0)
-        return (cur[r, lanes(p), :].astype(jnp.float32) + gates[r, lanes(p), :] * upd).astype(jnp.bfloat16)
+    def updated(t, cur, r, p, to):
+        for g in range(G):
+            y = precv[t, r * G + g, :, lanes(p)].astype(jnp.float32)
+            yn = norm(y, midg[t], 0)
+            upd = dot(yn, outw[t], 0, 0)
+            to[r * G + g, lanes(p), :] = (cur[r * G + g, lanes(p), :].astype(jnp.float32)
+                                          + gates[r * G + g, lanes(p), :] * upd).astype(jnp.bfloat16)
+
+    def finish(p):
+        wait_back(1, p)
+        def last(r):
+            updated(1, cur1, r, p, cur1)
+            cur = tokens(cur1, r, p)
+            xn = norm(cur, tgain[...], 1)
+            val = dot(xn, up[...], 1, 0)
+            q0, q1 = val[:, :hidden], val[:, hidden:]
+            h = (q0 * sigmoid(q0) * q1).astype(jnp.bfloat16)
+            out[pl.ds(r * G, G), lanes(p), :] = (cur + dot(h, down[...], 1, 0)).astype(jnp.bfloat16).reshape(G, LANES, C)
+        loop(R // G, last)
 
     for s in range(Q):
         project(0, pair, s)
         if s == 0:
             pl.semaphore_wait(barrier, N - 1)
         send_lr(0, s)
+        send_far(s)
     for s in range(Q):
         p = lax.rem(q + s, Q)
         def arrive(u, s=s, p=p):
@@ -157,40 +180,49 @@
         loop(M, arrive)
         def product(c):
             pT[c] = dot(lT[c], rT[c], 1, 1).astype(jnp.bfloat16)
-        loop(CB, product, 2)
+        loop(CB, product, 4)
         send_back(0, p)
-    for s in range(Q):
-        p = lax.rem(q + s, Q)
         wait_back(0, p)
         def row(r, p=p):
-            cur1[r, lanes(p), :] = updated(0, pair, r, p)
-        loop(R, row, 2)
+            updated(0, pair, r, p, cur1)
+        loop(R // G, row)
         project(1, cur1, p)
         send_lr(1, p)
-    def arrive1(u):
-        for h in range(Q):
-            pltpu.make_async_copy(rbuf.at[1, :, chans(u), lanes(h)], r1.at[rows(u, R), :, lanes(h)], r1r.at[u, h]).wait()
-            pltpu.make_async_copy(lbuf.at[1, :, chans(u), lanes(h)], l1.at[rows(u, R), :, lanes(h)], l1r.at[u, h]).wait()
-        rT[:, rows(u, R), :] = swap(r1[rows(u, R)])
-        lT[:, rows(u, R), :] = swap(l1[rows(u, R)])
-    loop(M, arrive1)
+
+    def left_here(p):
+        def one(u):
+            pltpu.make_async_copy(lbuf.at[1, :, chans(u), lanes(p)], l1.at[rows(u, R), :, lanes(p)], l1r.at[u, p]).wait()
+            lT[:, rows(u, R), lanes(p)] = swap(l1[rows(u, R), :, lanes(p)])
+        loop(M, one)
+
+    def right_here(p):
+        def one(u):
+            pltpu.make_async_copy(rbuf.at[1, :, chans(u), lanes(p)], r1.at[rows(u, R), :, lanes(p)], r1r.at[u, p]).wait()
+            rT[:, rows(u, R), lanes(p)] = swap(r1[rows(u, R), :, lanes(p)])
+        loop(M, one)
 
     def cross(d, p):
         return remote(xsend.at[d - 1, p], xrecv.at[d - 1, p], xs.at[d - 1, p], xr.at[d - 1, p],
                       lax.rem(q + d, Q) * M + m)
 
-    for p in range(Q):
+    left_here(q)
+    for s in range(Q):
+        p = lax.rem(q + s, Q)
+        right_here(p)
         for d in range(1, Q):
             other = lax.rem(q + d, Q)
+            if s == 0:
+                left_here(other)
             def partial(c, d=d, p=p, other=other):
                 xsend[d - 1, p, c] = dot(lT[c, :, lanes(other)], rT[c, :, lanes(p)], 0, 0).astype(jnp.bfloat16)
-            loop(CB, partial, 2)
+            loop(CB, partial, 4)
             cross(d, p).start()
     for p in range(Q):
         def mine(c, p=p):
             own[p, c] = dot(lT[c, :, lanes(q)], rT[c, :, lanes(p)], 0, 0)
-        loop(CB, mine, 2)
-    for p in range(Q):
+        loop(CB, mine, 4)
+    for s in range(Q):
+        p = lax.rem(q + 1 + s, Q)
         for d in range(1, Q):
             cross(d, p).wait_recv()
         def total(c, p=p):
@@ -200,16 +232,9 @@
             pT[c] = v.astype(jnp.bfloat16)
         loop(CB, total, 2)
         send_back(1, p)
-    for p in range(Q):
-        wait_back(1, p)
-        def last(r, p=p):
-            cur = updated(1, cur1, r, p).astype(jnp.float32)
-            xn = norm(cur, tgain[...], 1)
-            val = dot(xn, up[...], 1, 0)
-            q0, q1 = val[:, :hidden], val[:, hidden:]
-            h = (q0 * sigmoid(q0) * q1).astype(jnp.bfloat16)
-            out[r, lanes(p), :] = (cur + dot(h, down[...], 1, 0)).astype(jnp.bfloat16)
-        loop(R, last, 2)
+        if s > 0:
+            finish(lax.rem(q + s, Q))
+    finish(lax.rem(q + Q, Q))
     def drain(i):
         u = lax.rem(m + 1 + i, M)
         for p in range(Q):

time: 174 us -> 161 us (0.925); the launches traced: 174 us -> 159 us
  Pallas kernels: 168 us -> 153 us
    pallas_call x1, Pallas kernels: 168 us -> 153 us  [local(): pl.pallas_call(functools.partial(kernel, N, M, Q, R, roles), out_shape=ja...]
where the time goes in v2:
time: 161 us; the launch traced here: 159 us
  Pallas kernels  153 us (95%)
  local copies, waits for them, and re-layouts  5.56 us (3%)
    pallas_call x1, Pallas kernels, local(): pl.pallas_call(functools.partial(kernel, N, M, Q, R, roles), out_shape=ja...  153 us
    unnamed x4, local copies, waits for them, and re-layouts  4.76 us

profile of v2, /device:TPU:5, one launch (start us, length us, event | category | flops | bytes accessed | tf_op | source)
XLA Modules:
  0.0 158.8 jit_solution(5624023066191988899)
XLA Ops:
  0.0 0.0 copy-start
  0.0 0.7 copy-done
  0.7 0.8 copy.12.midg
  1.5 1.8 %copy.11 = bf16[2,128,512]{1,2,0:T(8,128)(2,1)} copy(bf16[2,128,512]{2,1,0:T(8,128)(2,1)} %param.11) | data formatting | bytes 524288 | tf_op args[2]
  3.3 153.3 %shard_map.91 = bf16[16,256,128]{2,1,0:T(8,128)(2,1)} custom-call(bf16[16,256,128]{2,1,0:T(8,128)(2,1)} %pair.1, f32[2,128]{1,0:T(2,128)} %gain.1, bf16[2,512,128]{2,1,0:T(8,128)(2,1)} %bitcast.3, bf16[2,128,128]{2,1,0:T(8,128)(2,1)} %gatew.1, f32[2,128,1]{2,1,0:T(8,128)} %copy.12.midg, bf16[2,128,128]{2,1,0:T(8,128)(2,1)} %outw.1, f32[1,128]{1,0:T(1,128)} %bitcast.5, ...), custom_call_target="tpu_custom_call" | custom-call | tf_op jit(solution)/shard_map/pallas_call | solution.py:270
  156.6 2.3 %copy.14 = bf16[16,256,128]{2,1,0:T(8,128)(2,1)} copy(bf16[16,256,128]{2,1,0:T(8,128)(2,1)} %shard_map.91) | data formatting | bytes 2097152
Async XLA Ops:
  0.0 0.7 copy-start

commit v3 on v2

--- a/solution.py
+++ b/solution.py
@@ -11,7 +11,9 @@
 MESH = pl.DeviceIdType.MESH
 LANES = 128
 G = 4
+KS = 2
 CB = 16
+KB = CB // KS
 
 
 def sigmoid(v):
@@ -96,22 +98,25 @@
         return remote(rbuf.at[t, :, chans(d), lanes(p)], r1.at[rows(src, R), :, lanes(p)],
                       r1s.at[d, p], r1r.at[src, p], q * M + d)
 
-    def self_copies(t, p):
+    def self_copy(side, t, p):
         dl, sl = (l0, lr) if t == 0 else (l1, l1r)
         dr, sr, at = (r0, rr, me) if t == 0 else (r1, r1r, m)
-        return (pltpu.make_async_copy(lbuf.at[t, :, chans(m), lanes(p)], dl.at[rows(m, R), :, lanes(p)], sl.at[m, p]),
-                pltpu.make_async_copy(rbuf.at[t, :, chans(m), lanes(p)], dr.at[rows(at, R), :, lanes(p)], sr.at[at, p]))
-
-    def send_lr(t, p):
-        for c in self_copies(t, p):
-            c.start()
-        def near_left(i):
+        if side == 0:
+            return pltpu.make_async_copy(lbuf.at[t, :, chans(m), lanes(p)], dl.at[rows(m, R), :, lanes(p)], sl.at[m, p])
+        return pltpu.make_async_copy(rbuf.at[t, :, chans(m), lanes(p)], dr.at[rows(at, R), :, lanes(p)], sr.at[at, p])
+
+    def send_left(t, p):
+        self_copy(0, t, p).start()
+        def near(i):
             left_copy(t, lax.rem(m + 1 + i, M), p, m).start()
-        def near_right(i):
+        loop(M - 1, near)
+
+    def send_right(t, p):
+        self_copy(1, t, p).start()
+        def near(i):
             u = lax.rem(m + 1 + i, M)
             right_copy(t, q * M + u if t == 0 else u, p, me if t == 0 else m).start()
-        loop(M - 1, near_left)
-        loop(M - 1, near_right)
+        loop(M - 1, near)
 
     def send_far(p):
         def far(i):
@@ -164,7 +169,9 @@
         project(0, pair, s)
         if s == 0:
             pl.semaphore_wait(barrier, N - 1)
-        send_lr(0, s)
+        send_left(0, s)
+        send_right(0, s)
+    for s in range(Q):
         send_far(s)
     for s in range(Q):
         p = lax.rem(q + s, Q)
@@ -187,7 +194,10 @@
             updated(0, pair, r, p, cur1)
         loop(R // G, row)
         project(1, cur1, p)
-        send_lr(1, p)
+        if s > 0:
+            send_left(1, p)
+        send_right(1, p)
+    send_left(1, q)
 
     def left_here(p):
         def one(u):
@@ -201,11 +211,10 @@
             rT[:, rows(u, R), lanes(p)] = swap(r1[rows(u, R), :, lanes(p)])
         loop(M, one)
 
-    def cross(d, p):
-        return remote(xsend.at[d - 1, p], xrecv.at[d - 1, p], xs.at[d - 1, p], xr.at[d - 1, p],
-                      lax.rem(q + d, Q) * M + m)
-
-    left_here(q)
+    def cross(d, p, k):
+        return remote(xsend.at[d - 1, p, k * KB : (k + 1) * KB], xrecv.at[d - 1, p, k * KB : (k + 1) * KB],
+                      xs.at[d - 1, p, k], xr.at[d - 1, p, k], lax.rem(q + d, Q) * M + m)
+
     for s in range(Q):
         p = lax.rem(q + s, Q)
         right_here(p)
@@ -213,24 +222,29 @@
             other = lax.rem(q + d, Q)
             if s == 0:
                 left_here(other)
-            def partial(c, d=d, p=p, other=other):
-                xsend[d - 1, p, c] = dot(lT[c, :, lanes(other)], rT[c, :, lanes(p)], 0, 0).astype(jnp.bfloat16)
-            loop(CB, partial, 4)
-            cross(d, p).start()
+            for k in range(KS):
+                def partial(i, d=d, p=p, other=other, k=k):
+                    c = k * KB + i
+                    xsend[d - 1, p, c] = dot(lT[c, :, lanes(other)], rT[c, :, lanes(p)], 0, 0).astype(jnp.bfloat16)
+                loop(KB, partial, 4)
+                cross(d, p, k).start()
+    left_here(q)
     for p in range(Q):
         def mine(c, p=p):
             own[p, c] = dot(lT[c, :, lanes(q)], rT[c, :, lanes(p)], 0, 0)
         loop(CB, mine, 4)
     for s in range(Q):
         p = lax.rem(q + 1 + s, Q)
-        for d in range(1, Q):
-            cross(d, p).wait_recv()
-        def total(c, p=p):
-            v = own[p, c]
+        for k in range(KS):
             for d in range(1, Q):
-                v = v + xrecv[d - 1, p, c].astype(jnp.float32)
-            pT[c] = v.astype(jnp.bfloat16)
-        loop(CB, total, 2)
+                cross(d, p, k).wait_recv()
+            def total(i, p=p, k=k):
+                c = k * KB + i
+                v = own[p, c]
+                for d in range(1, Q):
+                    v = v + xrecv[d - 1, p, c].astype(jnp.float32)
+                pT[c] = v.astype(jnp.bfloat16)
+            loop(KB, total, 2)
         send_back(1, p)
         if s > 0:
             finish(lax.rem(q + s, Q))
@@ -251,7 +265,8 @@
     loop(N - 1, drain_right)
     for p in range(Q):
         for d in range(1, Q):
-            cross(d, p).wait_send()
+            for k in range(KS):
+                cross(d, p, k).wait_send()
 
 
 def solution(mesh):
@@ -283,7 +298,7 @@
                 vm((Q, CB, part, LANES), f32),
                 dma((M, Q)), dma((M, Q)), dma((N, Q)), dma((N, Q)),
                 dma((M, Q)), dma((M, Q)), dma((M, Q)), dma((M, Q)),
-                dma((2, M, Q)), dma((2, M, Q)), dma((X, Q)), dma((X, Q)),
+                dma((2, M, Q)), dma((2, M, Q)), dma((X, Q, KS)), dma((X, Q, KS)),
             ],
             compiler_params=pltpu.CompilerParams(
                 collective_id=0, has_side_effects=True, vmem_limit_bytes=66_000_000),

time: 161 us -> 154 us (0.957)
  Pallas kernels: 153 us -> 148 us
    pallas_call x1, Pallas kernels: 153 us -> 148 us  [local(): pl.pallas_call(functools.partial(kernel, N, M, Q, R, roles), out_shape=ja...]
where the time goes in v3:
time: 154 us; the launch traced here: 153 us
  Pallas kernels  148 us (96%)
  local copies, waits for them, and re-layouts  5.56 us (4%)
    pallas_call x1, Pallas kernels, local(): pl.pallas_call(functools.partial(kernel, N, M, Q, R, roles), out_shape=ja...  148 us
    unnamed x4, local copies, waits for them, and re-layouts  4.76 us

profile of v3, /device:TPU:5, one launch (start us, length us, event | category | flops | bytes accessed | tf_op | source)
XLA Modules:
  0.0 153.4 jit_solution(2431060091327966442)
XLA Ops:
  0.0 0.0 copy-start
  0.0 0.7 copy-done
  0.7 0.8 copy.12.midg
  1.5 1.8 %copy.11 = bf16[2,128,512]{1,2,0:T(8,128)(2,1)} copy(bf16[2,128,512]{2,1,0:T(8,128)(2,1)} %param.11) | data formatting | bytes 524288 | tf_op args[2]
  3.3 147.8 %shard_map.91 = bf16[16,256,128]{2,1,0:T(8,128)(2,1)} custom-call(bf16[16,256,128]{2,1,0:T(8,128)(2,1)} %pair.1, f32[2,128]{1,0:T(2,128)} %gain.1, bf16[2,512,128]{2,1,0:T(8,128)(2,1)} %bitcast.3, bf16[2,128,128]{2,1,0:T(8,128)(2,1)} %gatew.1, f32[2,128,1]{2,1,0:T(8,128)} %copy.12.midg, bf16[2,128,128]{2,1,0:T(8,128)(2,1)} %outw.1, f32[1,128]{1,0:T(1,128)} %bitcast.5, ...), custom_call_target="tpu_custom_call" | custom-call | tf_op jit(solution)/shard_map/pallas_call | solution.py:285
  151.1 2.3 %copy.14 = bf16[16,256,128]{2,1,0:T(8,128)(2,1)} copy(bf16[16,256,128]{2,1,0:T(8,128)(2,1)} %shard_map.91) | data formatting | bytes 2097152
Async XLA Ops:
  0.0 0.7 copy-start

commit v4 on v3

--- a/solution.py
+++ b/solution.py
@@ -33,8 +33,9 @@
 
 def kernel(
     N, M, Q, R, roles,
-    pair, gain, projT, gatew, midg, outw, tgain, up, down, out,
+    pair, gain, proj, gatew, midg, outw, tgain, up, down, out,
     lbuf, rbuf, cur1, gates, l0, r0, l1, r1, lT, rT, pT, psend, precv, xsend, xrecv, own,
+    projT, midc,
     ls, lr, rs, rr, l1s, l1r, r1s, r1r, ps, pr, xs, xr,
 ):
     C = pair.shape[2]
@@ -74,6 +75,10 @@
 
     def tokens(cur, r, p):
         return cur[pl.ds(r * G, G), lanes(p), :].astype(jnp.float32).reshape(G * LANES, C)
+
+    def turn(t):
+        projT[t] = jnp.swapaxes(proj[t], 0, 1)
+        midc[t] = jnp.swapaxes(jnp.broadcast_to(midg[t : t + 1, :], (LANES, inner)), 0, 1)
 
     def project(t, cur, p):
         def row(r):
@@ -148,7 +153,7 @@
     def updated(t, cur, r, p, to):
         for g in range(G):
             y = precv[t, r * G + g, :, lanes(p)].astype(jnp.float32)
-            yn = norm(y, midg[t], 0)
+            yn = norm(y, midc[t], 0)
             upd = dot(yn, outw[t], 0, 0)
             to[r * G + g, lanes(p), :] = (cur[r * G + g, lanes(p), :].astype(jnp.float32)
                                           + gates[r * G + g, lanes(p), :] * upd).astype(jnp.bfloat16)
@@ -165,6 +170,7 @@
             out[pl.ds(r * G, G), lanes(p), :] = (cur + dot(h, down[...], 1, 0)).astype(jnp.bfloat16).reshape(G, LANES, C)
         loop(R // G, last)
 
+    turn(0)
     for s in range(Q):
         project(0, pair, s)
         if s == 0:
@@ -173,6 +179,7 @@
         send_right(0, s)
     for s in range(Q):
         send_far(s)
+    turn(1)
     for s in range(Q):
         p = lax.rem(q + s, Q)
         def arrive(u, s=s, p=p):
@@ -296,13 +303,14 @@
                 vm((2, Q, M, R, CB, LANES), bf), vm((2, R, inner, W), bf),
                 vm((X, Q, CB, part, LANES), bf), vm((X, Q, CB, part, LANES), bf),
                 vm((Q, CB, part, LANES), f32),
+                vm((2, tri_proj.shape[2], C), bf), vm((2, inner, LANES), f32),
                 dma((M, Q)), dma((M, Q)), dma((N, Q)), dma((N, Q)),
                 dma((M, Q)), dma((M, Q)), dma((M, Q)), dma((M, Q)),
                 dma((2, M, Q)), dma((2, M, Q)), dma((X, Q, KS)), dma((X, Q, KS)),
             ],
             compiler_params=pltpu.CompilerParams(
                 collective_id=0, has_side_effects=True, vmem_limit_bytes=66_000_000),
-        )(pair, tri_gain, jnp.swapaxes(tri_proj, 1, 2), tri_gate, tri_mid_gain[:, :, None], tri_out,
+        )(pair, tri_gain, tri_proj, tri_gate, tri_mid_gain, tri_out,
           trans_gain[None, :], trans_up, trans_down)
 
     in_specs = (P(("groups", "seq", "role"), None, None), P(), P(), P(), P(), P(), P(), P(), P())

time: 154 us -> 151 us (0.981)
  local copies, waits for them, and re-layouts: 5.56 us -> 2.3 us
    unnamed x4 -> x1, local copies, waits for them, and re-layouts: 4.76 us -> 2.3 us
where the time goes in v4:
time: 151 us; the launch traced here: 150 us
  Pallas kernels  148 us (98%)
  local copies, waits for them, and re-layouts  2.3 us (2%)
    pallas_call x1, Pallas kernels, local(): pl.pallas_call(functools.partial(kernel, N, M, Q, R, roles), out_shape=ja...  148 us

profile of v4, /device:TPU:5, one launch (start us, length us, event | category | flops | bytes accessed | tf_op | source)
XLA Modules:
  0.0 150.0 jit_solution(9751991779563378990)
XLA Ops:
  0.0 147.7 %shard_map.91 = bf16[16,256,128]{2,1,0:T(8,128)(2,1)} custom-call(bf16[16,256,128]{2,1,0:T(8,128)(2,1)} %pair.1, f32[2,128]{1,0:T(2,128)} %gain.1, bf16[2,128,512]{2,1,0:T(8,128)(2,1)} %proj.1, bf16[2,128,128]{2,1,0:T(8,128)(2,1)} %gatew.1, f32[2,128]{1,0:T(2,128)} %midg.1, bf16[2,128,128]{2,1,0:T(8,128)(2,1)} %outw.1, f32[1,128]{1,0:T(1,128)} %bitcast.1, ...), custom_call_target="tpu_custom_call" | custom-call | tf_op jit(solution)/shard_map/pallas_call | solution.py:292
  147.7 2.3 %copy.11 = bf16[16,256,128]{2,1,0:T(8,128)(2,1)} copy(bf16[16,256,128]{2,1,0:T(8,128)(2,1)} %shard_map.91) | data formatting | bytes 2097152
